TPU v7x, 32 devices: a whole 2x2x4 slice. The times are simulated.
32 devices in a mesh: groups: 1, seq: 16 (over z, y, core), head: 2 (over x).
Axes of the slice: x: 2, y: 2, z: 4, core: 2. Of those that a mesh axis runs over, the one named last changes fastest.
Arguments:
- x_proj: bfloat16 [12288, 8192], P(('groups', 'seq'), 'head'), may hold values from -6 to 6
- z_gate: bfloat16 [12288, 8192], P(('groups', 'seq'), 'head'), may hold values from -6 to 6
- bc_proj: bfloat16 [12288, 8, 256], P(('groups', 'seq'), 'head'), may hold values from -6 to 6
- dt_proj: bfloat16 [12288, 128], P(('groups', 'seq'), 'head'), may hold values from -5 to 5
- dt_bias: float32 [128], P('head'), may hold values from -4 to -1
- decay_log: float32 [128], P('head'), may hold values from -10 to 1
- skip_gain: float32 [128], P('head'), may hold values from 0.5 to 2
- conv_x: float32 [4, 8192], P(None, 'head'), may hold values from -3 to 3
- bias_x: float32 [8192], P('head'), may hold values from -3 to 3
- conv_bc: float32 [4, 8, 256], P(None, 'head'), may hold values from -3 to 3
- bias_bc: float32 [8, 256], P('head'), may hold values from -3 to 3
- norm_gain: float32 [8192], P('head'), may hold values from 0.5 to 1.5
- seg_lengths: int32 [4], P('groups'), may hold values from 1 to 6144, 12288 in all
Outputs:
- mixed: bfloat16 [12288, 8192], P(('groups', 'seq'), 'head')
Inputs may be any that keep to these rules, and one draw needn't show every extreme that they name: `seg_lengths`: the 4 rollouts fill the pack of 12288 tokens in order; the longest has exactly 6144 tokens.
All inputs are finite; a program needn't handle non-finite values.
Results may differ from a plain program's by a relative error of at most 0.0049.
Values may be sent and summed in bfloat16 or wider, within the bound.
A program may use at most 256 MiB of HBM per device.

v0:
```python
import functools

import jax
import jax.numpy as jnp
from jax import lax
from jax.experimental import pallas as pl
from jax.experimental.pallas import tpu as pltpu
from jax.sharding import PartitionSpec as P

HEAD_DIM = 64
STATE = 128
BLOCK = 128
LANES = 128
TAIL = 16
LOG2E = 1.4426950408889634
MESH = pl.DeviceIdType.MESH
F32 = jnp.float32
BF16 = jnp.bfloat16


def segment_of(seg_lengths, positions):
    starts = jnp.cumsum(seg_lengths) - seg_lengths
    hits = (starts[None, :] <= positions[:, None]).astype(jnp.int32)
    return jnp.sum(hits, axis=1) - 1


def silu(u):
    half = 0.5 * u
    return half + half * jnp.tanh(half)


def mm(a, b, dims, precision=None):
    return lax.dot_general(a, b, (dims, ((), ())), precision=precision, preferred_element_type=F32)


def steps_of(dtp_ref, dtb_ref, dec_ref):
    raw = dtp_ref[...].astype(F32) + dtb_ref[...]
    dt = jnp.maximum(raw, 0.0) + jnp.log1p(jnp.exp(-jnp.abs(raw)))
    la = (-LOG2E * jnp.exp(dec_ref[...])) * dt
    s = lax.broadcasted_iota(jnp.int32, (BLOCK, BLOCK), 0)
    t = lax.broadcasted_iota(jnp.int32, (BLOCK, BLOCK), 1)
    upper = (s <= t).astype(F32)
    return dt, mm(la, upper, ((1,), (0,)), lax.Precision.HIGHEST)


def expand(value, e_ref):
    hi = value.astype(BF16)
    lo = (value - hi.astype(F32)).astype(BF16)
    return mm(jnp.concatenate([hi, lo], axis=0), e_ref[...], ((0,), (0,)))


def conv_into(dst, src, tail, halo, weight, bias, masks, first):
    width = dst.shape[1]

    @pl.when(first)
    def _():
        halo[0:8, :] = tail[TAIL - 8 : TAIL, :].astype(F32)

    @pl.when(jnp.logical_not(first))
    def _():
        halo[0:8, :] = halo[BLOCK : BLOCK + 8, :]

    for j in range(width // LANES):
        sl = slice(j * LANES, (j + 1) * LANES)
        own = src[:, sl].astype(F32)
        halo[8 : BLOCK + 8, sl] = own
        total = bias[0:1, sl] + weight[3:4, sl] * own
        for k in range(3):
            total = total + weight[k : k + 1, sl] * (halo[5 + k : 5 + k + BLOCK, sl] * masks[k])
        dst[:, sl] = silu(total).astype(BF16)


def local_kernel(
    x_ref, xt_ref, bc_ref, bct_ref, dtp_ref, cols_ref, rows_ref, dtb_ref, dec_ref,
    wx_ref, bx_ref, wbc_ref, bbc_ref, e_ref,
    xc_ref, bcc_ref, s_ref, d_ref, xhalo, bhalo, scaled, tailw,
):
    b = pl.program_id(1)
    first = b == 0
    masks = [jnp.broadcast_to(cols_ref[:, k : k + 1], (BLOCK, LANES)) for k in range(3)]
    conv_into(xc_ref, x_ref, xt_ref, xhalo, wx_ref, bx_ref, masks, first)
    conv_into(bcc_ref, bc_ref, bct_ref, bhalo, wbc_ref, bbc_ref, masks, first)
    dt, cum = steps_of(dtp_ref, dtb_ref, dec_ref)
    last = cum[:, BLOCK - 1 : BLOCK]
    tailw[...] = expand(jnp.exp2(last - cum) * dt * rows_ref[0, 1:2, :], e_ref)
    decay = expand(jnp.exp2(jnp.broadcast_to(last, cum.shape)) * rows_ref[0, 3:4, :], e_ref)[0:8]
    width = x_ref.shape[1]
    for j in range(width // LANES):
        sl = slice(j * LANES, (j + 1) * LANES)
        scaled[:, sl] = (xc_ref[:, sl].astype(F32) * tailw[:, sl]).astype(BF16)
    update = mm(bcc_ref[:, 0:STATE], scaled[...], ((0,), (0,)))

    @pl.when(first)
    def _():
        s_ref[...] = update
        d_ref[...] = decay

    @pl.when(jnp.logical_not(first))
    def _():
        s_ref[...] = decay[0:1] * s_ref[...] + update
        d_ref[...] = decay * d_ref[...]


def chain_kernel(chunks, s_ref, d_ref, in_ref, sendbuf, recvbuf, send_sem, recv_sem):
    peers = lax.axis_size("seq")
    me = lax.axis_index("seq")
    width = s_ref.shape[1] // chunks
    barrier = pltpu.get_barrier_semaphore()

    for peer in (lax.rem(me + peers - 1, peers), lax.rem(me + 1, peers)):
        pl.semaphore_signal(barrier, inc=1, device_id={"seq": peer}, device_id_type=MESH)
    pl.semaphore_wait(barrier, 2)

    def copy(k):
        return pltpu.make_async_remote_copy(
            src_ref=sendbuf.at[k],
            dst_ref=recvbuf.at[k],
            send_sem=send_sem.at[k],
            recv_sem=recv_sem.at[k],
            device_id={"seq": lax.rem(me + 1, peers)},
            device_id_type=MESH,
        )

    for k in range(chunks):
        sl = slice(k * width, (k + 1) * width)

        @pl.when(me == 0)
        def _():
            in_ref[:, sl] = jnp.zeros((STATE, width), BF16)
            sendbuf[k] = s_ref[:, sl].astype(BF16)

        @pl.when(me > 0)
        def _():
            copy(k).wait_recv()
            arrived = recvbuf[k]
            in_ref[:, sl] = arrived
            sendbuf[k] = (d_ref[0:1, sl] * arrived.astype(F32) + s_ref[:, sl]).astype(BF16)

        @pl.when(me < peers - 1)
        def _():
            copy(k).start()

    for k in range(chunks):

        @pl.when(me < peers - 1)
        def _():
            copy(k).wait_send()


def output_kernel(
    xc_ref, bcc_ref, z_ref, in_ref, dtp_ref, cols_ref, rows_ref, dtb_ref, dec_ref,
    skip_ref, gain_ref, e_ref, out_ref, state, cfac, tailw, scaled, carried, gated,
):
    b = pl.program_id(1)
    width = xc_ref.shape[1]

    @pl.when(b == 0)
    def _():
        state[...] = in_ref[...].astype(F32)

    dt, cum = steps_of(dtp_ref, dtb_ref, dec_ref)
    cfac[...] = expand(jnp.exp2(cum) * rows_ref[0, 2:3, :], e_ref)
    last = cum[:, BLOCK - 1 : BLOCK]
    tailw[...] = expand(jnp.exp2(last - cum) * dt * rows_ref[0, 1:2, :], e_ref)
    b_part = bcc_ref[:, 0:STATE]
    c_part = bcc_ref[:, STATE : 2 * STATE]
    carried[...] = mm(c_part, state[...].astype(BF16), ((1,), (0,)))
    scores = mm(c_part, b_part, ((1,), (1,)))
    t = lax.broadcasted_iota(jnp.int32, (BLOCK, BLOCK), 0)
    s = lax.broadcasted_iota(jnp.int32, (BLOCK, BLOCK), 1)
    allowed = (s <= t) & (cols_ref[:, 3:4] == rows_ref[0, 0:1, :])
    scores = jnp.where(allowed, scores, 0.0)
    lower_rows = cum - jnp.log2(dt)
    columns = jnp.transpose(cum)
    lane = lax.broadcasted_iota(jnp.int32, (BLOCK, LANES), 1)
    left = lane < HEAD_DIM
    total = jnp.zeros((BLOCK, LANES), F32)
    for j in range(width // LANES):
        sl = slice(j * LANES, (j + 1) * LANES)
        parts = []
        for h in (2 * j, 2 * j + 1):
            spread = jnp.minimum(columns[:, h : h + 1] - lower_rows[h : h + 1, :], 80.0)
            parts.append((scores * jnp.exp2(spread)).astype(BF16))
        xc = xc_ref[:, sl]
        none = jnp.zeros_like(xc)
        pair = jnp.concatenate([jnp.where(left, xc, none), jnp.where(left, none, xc)], axis=0)
        y = mm(jnp.concatenate(parts, axis=1), pair, ((1,), (0,)))
        xf = xc.astype(F32)
        scaled[:, sl] = (xf * tailw[:, sl]).astype(BF16)
        full = y + cfac[:, sl] * carried[:, sl] + skip_ref[0:1, sl] * xf
        held = full * silu(z_ref[:, sl].astype(F32))
        gated[:, sl] = held
        total = total + held * held
    mean = jnp.sum(total, axis=1, keepdims=True) * (1.0 / width)
    scale = jnp.broadcast_to(lax.rsqrt(mean + 1e-05), (BLOCK, LANES))
    for j in range(width // LANES):
        sl = slice(j * LANES, (j + 1) * LANES)
        out_ref[:, sl] = (gated[:, sl] * scale * gain_ref[0:1, sl]).astype(BF16)

    @pl.when(b < pl.num_programs(1) - 1)
    def _():
        update = mm(b_part, scaled[...], ((0,), (0,)))
        state[...] = cfac[BLOCK - 1 : BLOCK, :] * state[...] + update


def shards(
    x_proj, z_gate, bc_proj, dt_proj, dt_bias, decay_log, skip_gain,
    conv_x, bias_x, conv_bc, bias_bc, norm_gain, seg_lengths,
):
    rows, channels = x_proj.shape
    lookback = conv_x.shape[0] - 1
    heads = dt_proj.shape[1]
    groups = bc_proj.shape[1]
    repeat = heads // groups
    wide = channels // groups
    blocks = rows // BLOCK
    peers = lax.axis_size("seq")
    bc = bc_proj.reshape(rows, groups * 2 * STATE)
    tails = jnp.concatenate([x_proj[rows - TAIL :], bc[rows - TAIL :]], axis=1)
    tails = lax.ppermute(tails, "seq", [(i, i + 1) for i in range(peers - 1)])
    x_tail, bc_tail = tails[:, :channels], tails[:, channels:]

    first_row = lax.axis_index("seq") * rows
    positions = first_row + jnp.arange(-lookback, rows, dtype=jnp.int32)
    segments = segment_of(seg_lengths, positions)
    own = segments[lookback:]
    columns = [(segments[k : k + rows] == own).astype(F32) for k in range(lookback)]
    columns = jnp.stack(columns + [own.astype(F32)] * (8 - lookback), axis=1)
    seg_blocks = own.reshape(blocks, BLOCK)
    before = segments[lookback - 1 :: BLOCK][:blocks]
    same_end = (seg_blocks == seg_blocks[:, -1:]).astype(F32)
    alive = (seg_blocks == before[:, None]).astype(F32)
    alive_end = jnp.broadcast_to(alive[:, -1:], alive.shape)
    lines = jnp.stack([seg_blocks.astype(F32), same_end, alive, alive_end] * 2, axis=1)

    dtp = dt_proj.T
    dtb = dt_bias[:, None]
    dec = decay_log[:, None]
    head_of = jnp.arange(wide)[None, :] // HEAD_DIM
    spread = (head_of == (jnp.arange(2 * repeat) % repeat)[:, None]).astype(BF16)

    def spec(shape, index):
        return pl.BlockSpec(shape, index)

    grid = (groups, blocks)
    tall = lambda w: spec((BLOCK, w), lambda g, b: (b, g))
    flat = lambda n, w: spec((n, w), lambda g, b: (0, g))
    shared = [
        spec((repeat, BLOCK), lambda g, b: (g, b)),
        spec((BLOCK, 8), lambda g, b: (b, 0)),
        spec((1, 8, BLOCK), lambda g, b: (b, 0, 0)),
        spec((repeat, 1), lambda g, b: (g, 0)),
        spec((repeat, 1), lambda g, b: (g, 0)),
    ]
    e_spec = spec((2 * repeat, wide), lambda g, b: (0, 0))
    params = pltpu.CompilerParams(
        dimension_semantics=("arbitrary", "arbitrary"), vmem_limit_bytes=48 << 20
    )
    xc, bcc, summary, decays = pl.pallas_call(
        local_kernel,
        grid=grid,
        in_specs=[
            tall(wide), flat(TAIL, wide), tall(2 * STATE), flat(TAIL, 2 * STATE), *shared,
            flat(lookback + 1, wide), flat(1, wide), flat(lookback + 1, 2 * STATE),
            flat(1, 2 * STATE), e_spec,
        ],
        out_specs=[tall(wide), tall(2 * STATE), flat(STATE, wide), flat(8, wide)],
        out_shape=[
            jax.ShapeDtypeStruct((rows, channels), BF16),
            jax.ShapeDtypeStruct((rows, groups * 2 * STATE), BF16),
            jax.ShapeDtypeStruct((STATE, channels), F32),
            jax.ShapeDtypeStruct((8, channels), F32),
        ],
        scratch_shapes=[
            pltpu.VMEM((BLOCK + 8, wide), F32),
            pltpu.VMEM((BLOCK + 8, 2 * STATE), F32),
            pltpu.VMEM((BLOCK, wide), BF16),
            pltpu.VMEM((BLOCK, wide), F32),
        ],
        compiler_params=params,
        name="local_state",
    )(
        x_proj, x_tail, bc, bc_tail, dtp, columns, lines, dtb, dec,
        conv_x, bias_x[None], conv_bc.reshape(lookback + 1, -1), bias_bc.reshape(1, -1), spread,
    )

    chunks = 16
    incoming = pl.pallas_call(
        functools.partial(chain_kernel, chunks),
        in_specs=[pl.BlockSpec(memory_space=pltpu.VMEM)] * 2,
        out_specs=pl.BlockSpec(memory_space=pltpu.VMEM),
        out_shape=jax.ShapeDtypeStruct((STATE, channels), BF16),
        scratch_shapes=[
            pltpu.VMEM((chunks, STATE, channels // chunks), BF16),
            pltpu.VMEM((chunks, STATE, channels // chunks), BF16),
            pltpu.SemaphoreType.DMA((chunks,)),
            pltpu.SemaphoreType.DMA((chunks,)),
        ],
        compiler_params=pltpu.CompilerParams(collective_id=0, has_side_effects=True),
        name="state_chain",
    )(summary, decays)

    big = pltpu.VMEM((BLOCK, wide), F32)
    return pl.pallas_call(
        output_kernel,
        grid=grid,
        in_specs=[
            tall(wide), tall(2 * STATE), tall(wide), flat(STATE, wide), *shared,
            flat(1, wide), flat(1, wide), e_spec,
        ],
        out_specs=tall(wide),
        out_shape=jax.ShapeDtypeStruct((rows, channels), BF16),
        scratch_shapes=[
            pltpu.VMEM((STATE, wide), F32), big, big, pltpu.VMEM((BLOCK, wide), BF16), big, big,
        ],
        compiler_params=params,
        name="block_outputs",
    )(
        xc, bcc, z_gate, incoming, dtp, columns, lines, dtb, dec,
        jnp.repeat(skip_gain, HEAD_DIM)[None], norm_gain[None], spread,
    )


def solution(mesh):
    return jax.shard_map(
        shards,
        mesh=mesh,
        in_specs=(
            P(("groups", "seq"), "head"),
            P(("groups", "seq"), "head"),
            P(("groups", "seq"), "head", None),
            P(("groups", "seq"), "head"),
            P("head"),
            P("head"),
            P("head"),
            P(None, "head"),
            P("head"),
            P(None, "head", None),
            P("head", None),
            P("head"),
            P("groups"),
        ),
        out_specs=P(("groups", "seq"), "head"),
        check_vma=False,
    )
```

profile of v0, /device:TPU:31, one launch (start us, length us, event | category | flops | bytes accessed | tf_op | source)
XLA Modules:
  0.0 150.5 jit_solution(10941645829382868200)
XLA Ops:
  0.0 0.8 slice.47
  0.8 0.9 slice.46
  1.7 1.3 collective-permute-start
  3.1 0.8 reduce-window.9
  3.9 0.7 bitcast_subtract_fusion
  5.1 1.3 copy.57
  6.8 0.7 copy.56
  7.5 1.4 copy.49.dtb_ref
  8.8 1.3 copy.50.dec_ref
  10.2 0.7 broadcast_in_dim.23
  10.9 0.7 broadcast_in_dim_reshape.3.skip_ref
  11.8 1.8 %copy.55 = bf16[96,8,4,256]{3,1,2,0:T(8,128)(2,1)S(1)} copy(bf16[96,8,4,256]{3,2,1,0:T(4,128)(2,1)} %bitcast.28) | data formatting | bytes 3145728
  13.7 0.6 stack.45.rows_ref
  14.4 0.9 copy-done.3
  15.3 0.8 copy-done.5
  16.1 0.8 copy-done.7
  16.8 0.7 copy-done.9
  17.6 0.8 copy-done.12
  18.4 0.7 copy-done.14
  19.1 0.7 copy-done.15
  19.8 39.0 %local_state.1 = (bf16[768,4096]{1,0:T(8,128)(2,1)}, bf16[768,1024]{1,0:T(8,128)(2,1)S(1)}, f32[128,4096]{1,0:T(8,128)}, f32[8,4096]{1,0:T(8,128)S(1)}) custom-call(bf16[768,4096]{1,0:T(8,128)(2,1)} %x_ref.1, bf16[16,4096]{1,0:T(8,128)(2,1)S(1)} %slice.63.xt_ref, bf16[768,1024]{1,0:T(8,128)(2,1)S(1)} %bitcast.21, bf16[16,1024]{1,0:T(8,128)(2,1)S(1)} %slice.64.bct_ref, ...), custom_call_target="tpu_custom_call" | custom-call | tf_op jit(solution)/shard_map/local_state/pallas_call | solution.py:259
  58.9 0.7 copy-done.11
  59.5 45.1 %state_chain.1.in_ref = bf16[128,4096]{1,0:T(8,128)(2,1)} custom-call(f32[128,4096]{1,0:T(8,128)} %get-tuple-element.11.s_ref, f32[8,4096]{1,0:T(8,128)} %copy-done.11), custom_call_target="tpu_custom_call" | custom-call | tf_op jit(solution)/shard_map/state_chain/pallas_call | solution.py:288
  104.7 1.2 copy-done
  105.9 0.8 copy-done.2
  106.7 0.9 copy-done.4
  107.6 0.8 copy-done.6
  108.4 0.8 copy-done.8
  109.1 0.7 copy-done.10
  109.9 0.7 copy-done.13
  110.6 0.7 copy-done.16
  111.3 39.2 %block_outputs.1 = bf16[768,4096]{1,0:T(8,128)(2,1)} custom-call(bf16[768,4096]{1,0:T(8,128)(2,1)} %get-tuple-element.9.xc_ref, bf16[768,1024]{1,0:T(8,128)(2,1)S(1)} %get-tuple-element.10.bcc_ref, bf16[768,4096]{1,0:T(8,128)(2,1)} %z_ref.1, bf16[128,4096]{1,0:T(8,128)(2,1)S(1)} %copy-done, bf16[64,768]{1,0:T(8,128)(2,1)S(1)} %bitcast.23, ...), custom_call_target="tpu_custom_call" | custom-call | tf_op jit(solution)/shard_map/block_outputs/pallas_call | solution.py:304
  (45 shorter events, 1.3 us)
Async XLA Ops:
  1.7 12.7 %collective-permute-start = (bf16[16,5120]{1,0:T(8,128)(2,1)S(1)}, bf16[16,5120]{1,0:T(8,128)(2,1)S(1)}, u32[]{:S(2)}, u32[]{:S(2)}) collective-permute-start(bf16[16,5120]{1,0:T(8,128)(2,1)S(1)} %pad_maximum_fusion), channel_id=1, source_target_pairs={{0,2},{2,4},{4,6},{6,8},{8,10},{10,12},{12,14},{14,16},{16,18},{18... | collective-permute-start | bytes 491528 | tf_op jit(solution)/shard_map/ppermute | solution.py:220
  14.4 44.5 %copy-start.1 = (bf16[32,1024]{1,0:T(8,128)(2,1)}, bf16[32,1024]{1,0:T(8,128)(2,1)S(1)}, u32[]{:S(2)}) copy-start(bf16[32,1024]{1,0:T(8,128)(2,1)S(1)} %compare_convert_fusion.e_ref) | copy-start | bytes 196612
  14.4 0.9 copy-start.3
  15.3 0.8 copy-start.5
  16.1 0.8 copy-start.7
  16.8 0.7 copy-start.9
  17.6 0.8 copy-start.12
  18.4 0.7 copy-start.14
  19.1 0.7 copy-start.15
  58.9 0.7 copy-start.11
  104.6 1.2 copy-start
  105.9 0.8 copy-start.2
  106.7 0.9 copy-start.4
  107.6 0.8 copy-start.6
  108.4 0.8 copy-start.8
  109.1 0.7 copy-start.10
  109.9 0.7 copy-start.13
  110.6 0.7 copy-start.16
where the time goes:
time: 152 us; the launch traced here: 151 us
  Pallas kernels  123 us (81%)
  local copies, waits for them, and re-layouts  23.5 us (15%)
  other arithmetic  2.17 us (1%)
    pallas_call x1, Pallas kernels, shards(): pl.pallas_call(functools.partial(chain_kernel, chunks), in_specs=[pl.Bloc...  45.1 us
    pallas_call x1, Pallas kernels, shards(): pl.pallas_call(output_kernel, grid=grid, in_specs=[tall(wide), tall(2 * S...  39.2 us
    pallas_call x1, Pallas kernels, shards(): pl.pallas_call(local_kernel, grid=grid, in_specs=[tall(wide), flat(TAIL,...  39 us
    unnamed x38, local copies, waits for them, and re-layouts  16.5 us
  transfers between devices with their start and end apart: 1, of which 0 were waited for; matrix products, arithmetic and copies ran while one was open for 7% of the time, Pallas kernels for 0%

commit v1 on v0

v1 whole, which is shorter than its diff:
```python
import functools

import jax
import jax.numpy as jnp
from jax import lax
from jax.experimental import pallas as pl
from jax.experimental.pallas import tpu as pltpu
from jax.sharding import PartitionSpec as P

HEAD_DIM = 64
STATE = 128
BLOCK = 128
LANES = 128
TAIL = 16
VMEM_LIMIT = 60 << 20
LOG2E = 1.4426950408889634
MESH = pl.DeviceIdType.MESH
F32 = jnp.float32
BF16 = jnp.bfloat16


def silu_of_half(half):
    return half + half * jnp.tanh(half)


def mm(a, b, dims, precision=None):
    return lax.dot_general(a, b, (dims, ((), ())), precision=precision, preferred_element_type=F32)


def ids_of(starts, positions):
    found = jnp.full(positions.shape, -1, jnp.int32)
    for start in starts:
        found = jnp.where(positions >= start, start, found)
    return found


def id_of(starts, position):
    found = jnp.int32(-1)
    for start in starts:
        found = jnp.where(position >= start, start, found)
    return found


class Spot:
    def __init__(self, seg_ref, block):
        rows = pl.num_programs(0) * BLOCK
        at = lax.axis_index("seq") * rows + block * BLOCK
        starts = [jnp.int32(0)]
        for j in range(seg_ref.shape[0] - 1):
            starts.append(starts[-1] + seg_ref[j])
        self.tall = at + lax.broadcasted_iota(jnp.int32, (BLOCK, LANES), 0)
        self.tall_id = ids_of(starts, self.tall)
        row = at + lax.broadcasted_iota(jnp.int32, (1, LANES), 1)
        self.row_id = ids_of(starts, row)
        before = id_of(starts, at - 1)
        end = id_of(starts, at + BLOCK - 1)
        self.same_end = (self.row_id == end).astype(F32)
        self.alive = (self.row_id == before).astype(F32)
        self.alive_end = (end == before).astype(F32)


def column(row):
    n = row.shape[1]
    i = lax.broadcasted_iota(jnp.int32, (n, n), 0)
    j = lax.broadcasted_iota(jnp.int32, (n, n), 1)
    return jnp.sum(jnp.where(i == j, row, 0.0), axis=1, keepdims=True)


def steps_of(dtp_ref, dtb_ref, dec_ref):
    raw = dtp_ref[...].astype(F32) + column(dtb_ref[...])
    dt = jnp.maximum(raw, 0.0) + jnp.log1p(jnp.exp(-jnp.abs(raw)))
    la = (-LOG2E * column(jnp.exp(dec_ref[...]))) * dt
    s = lax.broadcasted_iota(jnp.int32, (BLOCK, BLOCK), 0)
    t = lax.broadcasted_iota(jnp.int32, (BLOCK, BLOCK), 1)
    upper = (s <= t).astype(F32)
    return dt, mm(la, upper, ((1,), (0,)), lax.Precision.HIGHEST)


def fill_spread(e_ref):
    twice, wide = e_ref.shape
    row = lax.broadcasted_iota(jnp.int32, (twice, wide), 0)
    lane = lax.broadcasted_iota(jnp.int32, (twice, wide), 1)
    e_ref[...] = (lane // HEAD_DIM == row % (twice // 2)).astype(F32).astype(BF16)


def expand(value, e_ref):
    hi = value.astype(BF16)
    lo = (value - hi.astype(F32)).astype(BF16)
    return mm(jnp.concatenate([hi, lo], axis=0), e_ref[...], ((0,), (0,)))


def conv_tile(dst, src, halo, sl, weights, bias, masks):
    own = src[:, sl].astype(F32)
    halo[8 : BLOCK + 8, sl] = own
    total = 0.5 * bias + (0.5 * weights[3]) * own
    for k in range(3):
        total = total + (0.5 * weights[k]) * (halo[5 + k : 5 + k + BLOCK, sl] * masks[k])
    dst[:, sl] = silu_of_half(total).astype(BF16)


def tiles(start, width):
    return [slice(start + j, start + j + LANES) for j in range(0, width, LANES)]


def local_kernel(
    groups, seg_ref, x_ref, bc_ref, tail_ref, dtp_ref, dtb_ref, dec_ref,
    wx_ref, bx_ref, wbc_ref, bbc_ref,
    xc_ref, bcc_ref, s_ref, d_ref, xhalo, bhalo, scaled, e_ref,
):
    b = pl.program_id(0)
    channels = x_ref.shape[1]
    wide = channels // groups
    repeat = dtp_ref.shape[0] // groups

    @pl.when(b == 0)
    def _():
        fill_spread(e_ref)
        s_ref[...] = jnp.zeros(s_ref.shape, F32)
        d_ref[...] = jnp.ones(d_ref.shape, F32)
        xhalo[0:8, :] = tail_ref[TAIL - 8 : TAIL, 0:channels].astype(F32)
        bhalo[0:8, :] = tail_ref[TAIL - 8 : TAIL, channels:].astype(F32)

    @pl.when(b > 0)
    def _():
        xhalo[0:8, :] = xhalo[BLOCK : BLOCK + 8, :]
        bhalo[0:8, :] = bhalo[BLOCK : BLOCK + 8, :]

    spot = Spot(seg_ref, b)
    within = spot.tall - spot.tall_id
    masks = [(within >= 3 - k).astype(F32) for k in range(3)]
    dt, cum = steps_of(dtp_ref, dtb_ref, dec_ref)
    last = cum[:, BLOCK - 1 : BLOCK]
    tail_weight = jnp.exp2(last - cum) * dt * spot.same_end
    end_decay = jnp.exp2(jnp.broadcast_to(last, cum.shape)) * spot.alive_end
    for g in range(groups):
        heads = slice(g * repeat, (g + 1) * repeat)
        lanes = slice(g * wide, (g + 1) * wide)
        for j, sl in enumerate(tiles(g * 2 * STATE, 2 * STATE)):
            part = slice(j * LANES, (j + 1) * LANES)
            weights = [wbc_ref[k, g : g + 1, part] for k in range(4)]
            conv_tile(bcc_ref, bc_ref, bhalo, sl, weights, bbc_ref[g : g + 1, part], masks)
        tailw = expand(tail_weight[heads], e_ref)
        decay = expand(end_decay[heads], e_ref)[0:8]
        for j, sl in enumerate(tiles(g * wide, wide)):
            weights = [wx_ref[k : k + 1, sl] for k in range(4)]
            conv_tile(xc_ref, x_ref, xhalo, sl, weights, bx_ref[0:1, sl], masks)
            part = slice(j * LANES, (j + 1) * LANES)
            scaled[:, sl] = (xc_ref[:, sl].astype(F32) * tailw[:, part]).astype(BF16)
        b_part = bcc_ref[:, g * 2 * STATE : g * 2 * STATE + STATE]
        update = mm(b_part, scaled[:, lanes], ((0,), (0,)))
        s_ref[:, lanes] = decay[0:1] * s_ref[:, lanes] + update
        d_ref[:, lanes] = decay * d_ref[:, lanes]


def chain_kernel(
    chunks, s_ref, d_ref, in_ref, give, theirs, their_d, total, both_d, sendbuf, recvbuf, back,
    backed, give_sem, theirs_sem, send_sem, recv_sem, back_sem, backed_sem, d_sem,
):
    peers = lax.axis_size("seq")
    me = lax.axis_index("seq")
    core, link, links = lax.rem(me, 2), me // 2, peers // 2
    low = core == 0
    half = s_ref.shape[1] // 2
    width = half // chunks
    partner = me + 1 - 2 * core
    following = lax.rem(me + 2, peers)
    barrier = pltpu.get_barrier_semaphore()
    for peer in (partner, following, lax.rem(me + peers - 2, peers)):
        pl.semaphore_signal(barrier, inc=1, device_id={"seq": peer}, device_id_type=MESH)
    pl.semaphore_wait(barrier, 3)

    def piece(which, k):
        return pl.ds(pl.multiple_of(which * half + k * width, LANES), width)

    def copy(src, dst, sem, sem2, peer):
        return pltpu.make_async_remote_copy(
            src_ref=src, dst_ref=dst, send_sem=sem, recv_sem=sem2,
            device_id={"seq": peer}, device_id_type=MESH,
        )

    def give_copy(k):
        return copy(give.at[k], theirs.at[k], give_sem.at[k], theirs_sem.at[k], partner)

    def send_copy(k):
        return copy(sendbuf.at[k], recvbuf.at[k], send_sem.at[k], recv_sem.at[k], following)

    def back_copy(k):
        return copy(back.at[k], backed.at[k], back_sem.at[k], backed_sem.at[k], partner)

    d_copy = copy(d_ref, their_d, d_sem.at[0], d_sem.at[1], partner)
    d_copy.start()
    for k in range(chunks):
        give[k] = s_ref[:, piece(1 - core, k)].astype(BF16)
        give_copy(k).start()
    d_copy.wait()
    for k in range(chunks):
        give_copy(k).wait()
        mine, other = s_ref[:, piece(core, k)], theirs[k].astype(F32)
        d_mine, d_other = d_ref[0:1, piece(core, k)], their_d[0:1, piece(core, k)]
        d_late = jnp.where(low, d_other, d_mine)
        total[k] = d_late * jnp.where(low, mine, other) + jnp.where(low, other, mine)
        both_d[k] = jnp.broadcast_to(d_mine * d_other, (8, width))

        @pl.when(link == 0)
        def _():
            sendbuf[k] = total[k].astype(BF16)
            send_copy(k).start()

    for k in range(chunks):

        @pl.when(link == 0)
        def _():
            recvbuf[k] = jnp.zeros((STATE, width), BF16)

        @pl.when(link > 0)
        def _():
            send_copy(k).wait_recv()

        arrived = recvbuf[k].astype(F32)

        @pl.when((link > 0) & (link < links - 1))
        def _():
            sendbuf[k] = (both_d[k, 0:1] * arrived + total[k]).astype(BF16)
            send_copy(k).start()

        mine, other = s_ref[:, piece(core, k)], theirs[k].astype(F32)
        d_mine, d_other = d_ref[0:1, piece(core, k)], their_d[0:1, piece(core, k)]
        passed = jnp.where(low, d_mine, d_other) * arrived + jnp.where(low, mine, other)
        in_ref[:, piece(core, k)] = jnp.where(low, arrived, passed).astype(BF16)
        back[k] = jnp.where(low, passed, arrived).astype(BF16)
        back_copy(k).start()
    for k in range(chunks):
        back_copy(k).wait()
        in_ref[:, piece(1 - core, k)] = backed[k]

        @pl.when(link < links - 1)
        def _():
            send_copy(k).wait_send()


def output_kernel(
    groups, seg_ref, xc_ref, bcc_ref, z_ref, in_ref, dtp_ref, dtb_ref, dec_ref, skip_ref, gain_ref,
    out_ref, state, cfac, scaled, carried, gated, skip_row, e_ref,
):
    b = pl.program_id(0)
    channels = xc_ref.shape[1]
    wide = channels // groups
    repeat = dtp_ref.shape[0] // groups

    @pl.when(b == 0)
    def _():
        fill_spread(e_ref)
        state[...] = in_ref[...].astype(F32)
        skip = jnp.broadcast_to(column(skip_ref[...]), (groups * repeat, LANES))
        for g in range(groups):
            rows = skip[g * repeat : (g + 1) * repeat]
            skip_row[:, g * wide : (g + 1) * wide] = expand(rows, e_ref)[0:8]

    spot = Spot(seg_ref, b)
    dt, cum = steps_of(dtp_ref, dtb_ref, dec_ref)
    carry_weight = jnp.exp2(cum) * spot.alive
    last = cum[:, BLOCK - 1 : BLOCK]
    tail_weight = jnp.exp2(last - cum) * dt * spot.same_end
    lower_rows = cum - jnp.log2(dt)
    columns = jnp.transpose(cum)
    t = lax.broadcasted_iota(jnp.int32, (BLOCK, BLOCK), 0)
    s = lax.broadcasted_iota(jnp.int32, (BLOCK, BLOCK), 1)
    allowed = (s <= t) & (spot.tall_id == spot.row_id)
    lane = lax.broadcasted_iota(jnp.int32, (BLOCK, LANES), 1)
    left = lane < HEAD_DIM
    for g in range(groups):
        heads = slice(g * repeat, (g + 1) * repeat)
        lanes = slice(g * wide, (g + 1) * wide)
        cfac[:, lanes] = expand(carry_weight[heads], e_ref)
        tailw = expand(tail_weight[heads], e_ref)
        b_part = bcc_ref[:, g * 2 * STATE : g * 2 * STATE + STATE]
        c_part = bcc_ref[:, g * 2 * STATE + STATE : (g + 1) * 2 * STATE]
        carried[:, lanes] = mm(c_part, state[:, lanes].astype(BF16), ((1,), (0,)))
        scores = jnp.where(allowed, mm(c_part, b_part, ((1,), (1,))), 0.0)
        squares = jnp.zeros((BLOCK, LANES), F32)
        for j, sl in enumerate(tiles(g * wide, wide)):
            parts = []
            for h in (g * repeat + 2 * j, g * repeat + 2 * j + 1):
                spread = jnp.minimum(columns[:, h : h + 1] - lower_rows[h : h + 1, :], 80.0)
                parts.append((scores * jnp.exp2(spread)).astype(BF16))
            xc = xc_ref[:, sl]
            none = jnp.zeros_like(xc)
            pair = jnp.concatenate([jnp.where(left, xc, none), jnp.where(left, none, xc)], axis=0)
            y = mm(jnp.concatenate(parts, axis=1), pair, ((1,), (0,)))
            xf = xc.astype(F32)
            scaled[:, sl] = (xf * tailw[:, j * LANES : (j + 1) * LANES]).astype(BF16)
            full = y + cfac[:, sl] * carried[:, sl] + skip_row[0:1, sl] * xf
            held = full * silu_of_half(0.5 * z_ref[:, sl].astype(F32))
            gated[:, sl] = held
            squares = squares + held * held
        mean = jnp.sum(squares, axis=1, keepdims=True) * (1.0 / wide)
        scale = jnp.broadcast_to(lax.rsqrt(mean + 1e-05), (BLOCK, LANES))
        for sl in tiles(g * wide, wide):
            out_ref[:, sl] = (gated[:, sl] * scale * gain_ref[0:1, sl]).astype(BF16)
        update = mm(b_part, scaled[:, lanes], ((0,), (0,)))
        state[:, lanes] = cfac[BLOCK - 1 : BLOCK, lanes] * state[:, lanes] + update


def shards(
    x_proj, z_gate, bc_proj, dt_proj, dt_bias, decay_log, skip_gain,
    conv_x, bias_x, conv_bc, bias_bc, norm_gain, seg_lengths,
):
    rows, channels = x_proj.shape
    lookback = conv_x.shape[0] - 1
    heads = dt_proj.shape[1]
    groups = bc_proj.shape[1]
    repeat = heads // groups
    wide = channels // groups
    blocks = rows // BLOCK
    peers = lax.axis_size("seq")
    bc = bc_proj.reshape(rows, groups * 2 * STATE)
    tails = jnp.concatenate([x_proj[rows - TAIL :], bc[rows - TAIL :]], axis=1)
    tails = lax.ppermute(tails, "seq", [(i, i + 1) for i in range(peers - 1)])
    dtp = dt_proj.T
    tall = lambda w: pl.BlockSpec((BLOCK, w), lambda b: (b, 0))
    whole = lambda *shape: pl.BlockSpec(shape, lambda b: (0,) * len(shape))
    lengths = pl.BlockSpec(memory_space=pltpu.SMEM)
    scalars = [pl.BlockSpec((heads, BLOCK), lambda b: (0, b)), whole(1, heads), whole(1, heads)]
    params = pltpu.CompilerParams(
        dimension_semantics=("arbitrary",), vmem_limit_bytes=VMEM_LIMIT
    )
    pairs = groups * 2 * STATE
    xc, bcc, summary, decays = pl.pallas_call(
        functools.partial(local_kernel, groups),
        grid=(blocks,),
        in_specs=[
            lengths, tall(channels), tall(pairs), whole(TAIL, channels + pairs), *scalars,
            whole(lookback + 1, channels), whole(1, channels),
            whole(lookback + 1, groups, 2 * STATE), whole(groups, 2 * STATE),
        ],
        out_specs=[tall(channels), tall(pairs), whole(STATE, channels), whole(8, channels)],
        out_shape=[
            jax.ShapeDtypeStruct((rows, channels), BF16),
            jax.ShapeDtypeStruct((rows, pairs), BF16),
            jax.ShapeDtypeStruct((STATE, channels), F32),
            jax.ShapeDtypeStruct((8, channels), F32),
        ],
        scratch_shapes=[
            pltpu.VMEM((BLOCK + 8, channels), F32),
            pltpu.VMEM((BLOCK + 8, pairs), F32),
            pltpu.VMEM((BLOCK, channels), BF16),
            pltpu.VMEM((2 * repeat, wide), BF16),
        ],
        compiler_params=params,
        name="local_state",
    )(
        seg_lengths, x_proj, bc, tails, dtp, dt_bias[None], decay_log[None],
        conv_x, bias_x[None], conv_bc, bias_bc,
    )

    chunks = 16
    width = channels // 2 // chunks
    pieces = pltpu.VMEM((chunks, STATE, width), BF16)
    sems = pltpu.SemaphoreType.DMA((chunks,))
    incoming = pl.pallas_call(
        functools.partial(chain_kernel, chunks),
        in_specs=[pl.BlockSpec(memory_space=pltpu.VMEM)] * 2,
        out_specs=pl.BlockSpec(memory_space=pltpu.VMEM),
        out_shape=jax.ShapeDtypeStruct((STATE, channels), BF16),
        scratch_shapes=[
            pieces, pieces, pltpu.VMEM((8, channels), F32),
            pltpu.VMEM((chunks, STATE, width), F32), pltpu.VMEM((chunks, 8, width), F32),
            pieces, pieces, pieces, pieces,
            sems, sems, sems, sems, sems, sems, pltpu.SemaphoreType.DMA((2,)),
        ],
        compiler_params=pltpu.CompilerParams(
            collective_id=0, has_side_effects=True, vmem_limit_bytes=VMEM_LIMIT
        ),
        name="state_chain",
    )(summary, decays)

    big = pltpu.VMEM((BLOCK, channels), F32)
    return pl.pallas_call(
        functools.partial(output_kernel, groups),
        grid=(blocks,),
        in_specs=[
            lengths, tall(channels), tall(pairs), tall(channels), whole(STATE, channels), *scalars,
            whole(1, heads), whole(1, channels),
        ],
        out_specs=tall(channels),
        out_shape=jax.ShapeDtypeStruct((rows, channels), BF16),
        scratch_shapes=[
            pltpu.VMEM((STATE, channels), F32), big, pltpu.VMEM((BLOCK, channels), BF16), big, big,
            pltpu.VMEM((8, channels), F32), pltpu.VMEM((2 * repeat, wide), BF16),
        ],
        compiler_params=params,
        name="block_outputs",
    )(
        seg_lengths, xc, bcc, z_gate, incoming, dtp, dt_bias[None], decay_log[None],
        skip_gain[None], norm_gain[None],
    )


def solution(mesh):
    return jax.shard_map(
        shards,
        mesh=mesh,
        in_specs=(
            P(("groups", "seq"), "head"),
            P(("groups", "seq"), "head"),
            P(("groups", "seq"), "head", None),
            P(("groups", "seq"), "head"),
            P("head"),
            P("head"),
            P("head"),
            P(None, "head"),
            P("head"),
            P(None, "head", None),
            P("head", None),
            P("head"),
            P("groups"),
        ),
        out_specs=P(("groups", "seq"), "head"),
        check_vma=False,
    )
```

time: 152 us -> 103 us (0.68); the launches traced: 151 us -> 103 us
  Pallas kernels: 123 us -> 96.4 us
  local copies, waits for them, and re-layouts: 23.5 us -> 5.37 us
  other arithmetic: 2.17 us -> 0.01 us
    pallas_call x2, Pallas kernels: 78.3 us -> 53.4 us  [the longest x1 27 us: shards(): pl.pallas_call(functools.partial(output_kernel, groups), grid=(blocks,),...]
    unnamed x38 -> x4, local copies, waits for them, and re-layouts: 16.5 us -> 3.68 us
    broadcast_in_dim x3 -> x0, local copies, waits for them, and re-layouts: 3.43 us -> none  [the longest x1 1.35 us: shards(): dtb = dt_bias[:, None]]
    pallas_call x1, Pallas kernels: 45.1 us -> 43 us  [shards(): pl.pallas_call(functools.partial(chain_kernel, chunks), in_specs=[pl.Bloc...]
    another operation x9 -> x0, local copies, waits for them, and re-layouts: 1.62 us -> none  [the longest x2 0.72 us: shards(): jnp.stack([seg_blocks.astype(F32), same_end, alive, alive_end] * 2, axis=1)]
  transfers between devices with their start and end apart: 1 -> 1, of which waited for: 0 -> 0; matrix products, arithmetic and copies ran while one was open for 7% -> 3% of each run, Pallas kernels for 0% -> 0%
where the time goes in v1:
time: 103 us
  Pallas kernels  96.4 us (94%)
  local copies, waits for them, and re-layouts  5.37 us (5%)
  starting transfers between devices  1.29 us (1%)
    pallas_call x1, Pallas kernels, shards(): pl.pallas_call(functools.partial(chain_kernel, chunks), in_specs=[pl.Bloc...  43 us
    pallas_call x1, Pallas kernels, shards(): pl.pallas_call(functools.partial(output_kernel, groups), grid=(blocks,),...  27 us
    pallas_call x1, Pallas kernels, shards(): pl.pallas_call(functools.partial(local_kernel, groups), grid=(blocks,), i...  26.4 us
    unnamed x4, local copies, waits for them, and re-layouts  3.68 us
  transfers between devices with their start and end apart: 1, of which 0 were waited for; matrix products, arithmetic and copies ran while one was open for 3% of the time, Pallas kernels for 0%

profile of v1, /device:TPU:31, one launch (start us, length us, event | category | flops | bytes accessed | tf_op | source)
XLA Modules:
  0.0 103.1 jit_solution(9358015752383343887)
XLA Ops:
  0.0 0.8 slice.10
  0.8 0.9 slice.9
  1.7 1.3 %collective-permute-start = (bf16[16,5120]{1,0:T(8,128)(2,1)S(1)}, bf16[16,5120]{1,0:T(8,128)(2,1)S(1)}, u32[]{:S(2)}, u32[]{:S(2)}) collective-permute-start(bf16[16,5120]{1,0:T(8,128)(2,1)S(1)} %pad_maximum_fusion), channel_id=1, source_target_pairs={{0,2},{2,4},{4,6},{6,8},{8,10},{10,12},{12,14},{14,16},{16,18},{18... | collective-permute-start | bytes 491528 | tf_op jit(solution)/shard_map/ppermute | solution.py:318
  3.0 3.0 %copy.14 = bf16[96,8,4,256]{3,1,2,0:T(8,128)(2,1)} copy(bf16[96,8,4,256]{3,2,1,0:T(4,128)(2,1)} %bitcast.11) | data formatting | bytes 3145728
  6.0 0.0 collective-permute-done.tail_ref
  6.0 0.0 copy-start
  6.0 0.7 copy-done
  6.7 26.4 %local_state.1 = (bf16[768,4096]{1,0:T(8,128)(2,1)}, bf16[768,1024]{1,0:T(8,128)(2,1)}, f32[128,4096]{1,0:T(8,128)}, f32[8,4096]{1,0:T(8,128)}) custom-call(s32[4]{0:T(128)} %seg_ref.3, bf16[768,4096]{1,0:T(8,128)(2,1)} %x_ref.1, bf16[768,1024]{1,0:T(8,128)(2,1)} %bitcast.10, bf16[16,5120]{1,0:T(8,128)(2,1)} %copy-done, bf16[64,768]{1,0:T(8,128)(2,1)} %bitcast.12, ...), custom_call_target="tpu_custom_call" | custom-call | tf_op jit(solution)/shard_map/local_state/pallas_call | solution.py:328
  33.1 43.0 %state_chain.1.in_ref = bf16[128,4096]{1,0:T(8,128)(2,1)} custom-call(f32[128,4096]{1,0:T(8,128)} %get-tuple-element.11.s_ref, f32[8,4096]{1,0:T(8,128)} %get-tuple-element.12.d_ref), custom_call_target="tpu_custom_call" | custom-call | tf_op jit(solution)/shard_map/state_chain/pallas_call | solution.py:360
  76.1 27.0 %block_outputs.1 = bf16[768,4096]{1,0:T(8,128)(2,1)} custom-call(s32[4]{0:T(128)} %seg_ref.3, bf16[768,4096]{1,0:T(8,128)(2,1)} %get-tuple-element.9.xc_ref, bf16[768,1024]{1,0:T(8,128)(2,1)} %get-tuple-element.10.bcc_ref, bf16[768,4096]{1,0:T(8,128)(2,1)} %z_ref.1, bf16[128,4096]{1,0:T(8,128)(2,1)} %state_chain.1.in_ref, bf16[64,768]{1,0:T(8,128)(2,1)} %bitcast.13, ...), custom_call_target="tpu_custom_call" | custom-call | tf_op jit(solution)/shard_map/block_outputs/pallas_call | solution.py:378
  (2 shorter events, 0.0 us)
Async XLA Ops:
  1.7 4.3 %collective-permute-start = (bf16[16,5120]{1,0:T(8,128)(2,1)S(1)}, bf16[16,5120]{1,0:T(8,128)(2,1)S(1)}, u32[]{:S(2)}, u32[]{:S(2)}) collective-permute-start(bf16[16,5120]{1,0:T(8,128)(2,1)S(1)} %pad_maximum_fusion), channel_id=1, source_target_pairs={{0,2},{2,4},{4,6},{6,8},{8,10},{10,12},{12,14},{14,16},{16,18},{18... | collective-permute-start | bytes 491528 | tf_op jit(solution)/shard_map/ppermute | solution.py:318
  6.0 0.7 copy-start

commit v2 on v1

--- a/solution.py
+++ b/solution.py
@@ -89,13 +89,23 @@
     return mm(jnp.concatenate([hi, lo], axis=0), e_ref[...], ((0,), (0,)))
 
 
-def conv_tile(dst, src, halo, sl, weights, bias, masks):
-    own = src[:, sl].astype(F32)
-    halo[8 : BLOCK + 8, sl] = own
-    total = 0.5 * bias + (0.5 * weights[3]) * own
+def shift_matrix(within):
+    t = lax.broadcasted_iota(jnp.int32, (BLOCK, TAIL + BLOCK), 0)
+    i = lax.broadcasted_iota(jnp.int32, (BLOCK, TAIL + BLOCK), 1)
+    steps = [((i == t + (TAIL - 3 + k)) & (within[:, 0:1] >= 3 - k)).astype(F32) for k in range(3)]
+    return jnp.concatenate(steps, axis=0).astype(BF16)
+
+
+def conv_tile(dst, halo, shift, cols, out, weights, bias):
+    src = halo[:, cols]
+    past = mm(shift, src, ((1,), (0,)))
+    own = src[TAIL:, :].astype(F32)
+    half = 0.5 * bias + (0.5 * weights[3]) * own
     for k in range(3):
-        total = total + (0.5 * weights[k]) * (halo[5 + k : 5 + k + BLOCK, sl] * masks[k])
-    dst[:, sl] = silu_of_half(total).astype(BF16)
+        half = half + (0.5 * weights[k]) * past[k * BLOCK : (k + 1) * BLOCK]
+    value = silu_of_half(half).astype(BF16)
+    dst[:, out] = value
+    return value
 
 
 def tiles(start, width):
@@ -117,17 +127,18 @@
         fill_spread(e_ref)
         s_ref[...] = jnp.zeros(s_ref.shape, F32)
         d_ref[...] = jnp.ones(d_ref.shape, F32)
-        xhalo[0:8, :] = tail_ref[TAIL - 8 : TAIL, 0:channels].astype(F32)
-        bhalo[0:8, :] = tail_ref[TAIL - 8 : TAIL, channels:].astype(F32)
+        xhalo[0:TAIL, :] = tail_ref[:, 0:channels]
+        bhalo[0:TAIL, :] = tail_ref[:, channels:]
 
     @pl.when(b > 0)
     def _():
-        xhalo[0:8, :] = xhalo[BLOCK : BLOCK + 8, :]
-        bhalo[0:8, :] = bhalo[BLOCK : BLOCK + 8, :]
-
+        xhalo[0:TAIL, :] = xhalo[BLOCK : BLOCK + TAIL, :]
+        bhalo[0:TAIL, :] = bhalo[BLOCK : BLOCK + TAIL, :]
+
+    xhalo[TAIL:, :] = x_ref[...]
+    bhalo[TAIL:, :] = bc_ref[...]
     spot = Spot(seg_ref, b)
-    within = spot.tall - spot.tall_id
-    masks = [(within >= 3 - k).astype(F32) for k in range(3)]
+    shift = shift_matrix(spot.tall - spot.tall_id)
     dt, cum = steps_of(dtp_ref, dtb_ref, dec_ref)
     last = cum[:, BLOCK - 1 : BLOCK]
     tail_weight = jnp.exp2(last - cum) * dt * spot.same_end
@@ -135,17 +146,16 @@
     for g in range(groups):
         heads = slice(g * repeat, (g + 1) * repeat)
         lanes = slice(g * wide, (g + 1) * wide)
-        for j, sl in enumerate(tiles(g * 2 * STATE, 2 * STATE)):
-            part = slice(j * LANES, (j + 1) * LANES)
-            weights = [wbc_ref[k, g : g + 1, part] for k in range(4)]
-            conv_tile(bcc_ref, bc_ref, bhalo, sl, weights, bbc_ref[g : g + 1, part], masks)
+        sl = slice(g * 2 * STATE, (g + 1) * 2 * STATE)
+        weights = [wbc_ref[k, g : g + 1, :] for k in range(4)]
+        conv_tile(bcc_ref, bhalo, shift, sl, sl, weights, bbc_ref[g : g + 1, :])
         tailw = expand(tail_weight[heads], e_ref)
         decay = expand(end_decay[heads], e_ref)[0:8]
-        for j, sl in enumerate(tiles(g * wide, wide)):
+        for j in range(0, wide, 2 * LANES):
+            sl = slice(g * wide + j, g * wide + j + 2 * LANES)
             weights = [wx_ref[k : k + 1, sl] for k in range(4)]
-            conv_tile(xc_ref, x_ref, xhalo, sl, weights, bx_ref[0:1, sl], masks)
-            part = slice(j * LANES, (j + 1) * LANES)
-            scaled[:, sl] = (xc_ref[:, sl].astype(F32) * tailw[:, part]).astype(BF16)
+            value = conv_tile(xc_ref, xhalo, shift, sl, sl, weights, bx_ref[0:1, sl])
+            scaled[:, sl] = (value.astype(F32) * tailw[:, j : j + 2 * LANES]).astype(BF16)
         b_part = bcc_ref[:, g * 2 * STATE : g * 2 * STATE + STATE]
         update = mm(b_part, scaled[:, lanes], ((0,), (0,)))
         s_ref[:, lanes] = decay[0:1] * s_ref[:, lanes] + update
@@ -153,89 +163,138 @@
 
 
 def chain_kernel(
-    chunks, s_ref, d_ref, in_ref, give, theirs, their_d, total, both_d, sendbuf, recvbuf, back,
-    backed, give_sem, theirs_sem, send_sem, recv_sem, back_sem, backed_sem, d_sem,
+    chunks, s_ref, d_ref, in_ref, give1, take1, give2, take2, total1, total2, sent, arrive,
+    back2, home2, back1, home1, hold_d1, both_d1, hold_d2, both_d2, sem1, sem2, sem3, sem4, sem5, dsem,
 ):
     peers = lax.axis_size("seq")
     me = lax.axis_index("seq")
-    core, link, links = lax.rem(me, 2), me // 2, peers // 2
-    low = core == 0
+    core, pair, link, links = lax.rem(me, 2), lax.rem(me // 2, 2), me // 4, peers // 4
+    low1, low2 = core == 0, pair == 0
     half = s_ref.shape[1] // 2
-    width = half // chunks
-    partner = me + 1 - 2 * core
-    following = lax.rem(me + 2, peers)
+    quarter = half // 2
+    width = quarter // chunks
+    near, far = me + 1 - 2 * core, me + 2 - 4 * pair
+    following = lax.rem(me + 4, peers)
     barrier = pltpu.get_barrier_semaphore()
-    for peer in (partner, following, lax.rem(me + peers - 2, peers)):
+    for peer in (near, far, following, lax.rem(me + peers - 4, peers)):
         pl.semaphore_signal(barrier, inc=1, device_id={"seq": peer}, device_id_type=MESH)
-    pl.semaphore_wait(barrier, 3)
-
-    def piece(which, k):
+    pl.semaphore_wait(barrier, 4)
+
+    def lanes(which, k):
         return pl.ds(pl.multiple_of(which * half + k * width, LANES), width)
 
-    def copy(src, dst, sem, sem2, peer):
+    def inner(k):
+        return pl.ds(pl.multiple_of(k * width, LANES), width)
+
+    def copy(src, dst, sems, peer):
         return pltpu.make_async_remote_copy(
-            src_ref=src, dst_ref=dst, send_sem=sem, recv_sem=sem2,
+            src_ref=src, dst_ref=dst, send_sem=sems.at[0], recv_sem=sems.at[1],
             device_id={"seq": peer}, device_id_type=MESH,
         )
 
-    def give_copy(k):
-        return copy(give.at[k], theirs.at[k], give_sem.at[k], theirs_sem.at[k], partner)
-
-    def send_copy(k):
-        return copy(sendbuf.at[k], recvbuf.at[k], send_sem.at[k], recv_sem.at[k], following)
-
-    def back_copy(k):
-        return copy(back.at[k], backed.at[k], back_sem.at[k], backed_sem.at[k], partner)
-
-    d_copy = copy(d_ref, their_d, d_sem.at[0], d_sem.at[1], partner)
-    d_copy.start()
-    for k in range(chunks):
-        give[k] = s_ref[:, piece(1 - core, k)].astype(BF16)
-        give_copy(k).start()
-    d_copy.wait()
-    for k in range(chunks):
-        give_copy(k).wait()
-        mine, other = s_ref[:, piece(core, k)], theirs[k].astype(F32)
-        d_mine, d_other = d_ref[0:1, piece(core, k)], their_d[0:1, piece(core, k)]
-        d_late = jnp.where(low, d_other, d_mine)
-        total[k] = d_late * jnp.where(low, mine, other) + jnp.where(low, other, mine)
-        both_d[k] = jnp.broadcast_to(d_mine * d_other, (8, width))
+    def copy1(k):
+        return copy(give1.at[k], take1.at[k], sem1.at[k], near)
+
+    def copy2(k):
+        return copy(give2.at[k], take2.at[k], sem2.at[k], far)
+
+    def copy3(k):
+        return copy(sent.at[k], arrive.at[k], sem3.at[k], following)
+
+    def copy4(k):
+        return copy(back2.at[k], home2.at[k], sem4.at[k], far)
+
+    def copy5(k):
+        return copy(back1.at[k], home1.at[k], sem5.at[k], near)
+
+    def half_lanes(which):
+        return pl.ds(pl.multiple_of(which * half, LANES), half)
+
+    def quarter_lanes(which):
+        return pl.ds(pl.multiple_of(which * quarter, LANES), quarter)
+
+    dcopy1 = copy(d_ref.at[:, half_lanes(1 - core)], hold_d1, dsem.at[0], near)
+    dcopy2 = copy(both_d1.at[:, quarter_lanes(1 - pair)], hold_d2, dsem.at[1], far)
+    dcopy1.start()
+    theirs, ours = (1 - pair) * chunks, pair * chunks
+    order = [theirs + k for k in range(chunks)] + [ours + k for k in range(chunks)]
+    for k in order:
+        give1[k] = s_ref[:, lanes(1 - core, k)].astype(BF16)
+        copy1(k).start()
+    dcopy1.wait()
+    both_d1[...] = d_ref[:, half_lanes(core)] * hold_d1[...]
+    dcopy2.start()
+
+    def merge1(k):
+        copy1(k).wait()
+        mine, other = s_ref[:, lanes(core, k)], take1[k].astype(F32)
+        d_late = jnp.where(low1, hold_d1[0:1, inner(k)], d_ref[0:1, lanes(core, k)])
+        return d_late * jnp.where(low1, mine, other) + jnp.where(low1, other, mine)
+
+    for k in range(chunks):
+        give2[k] = merge1(theirs + k).astype(BF16)
+        copy2(k).start()
+    for k in range(chunks):
+        total1[k] = merge1(ours + k)
+    dcopy2.wait()
+    both_d2[...] = both_d1[:, quarter_lanes(pair)] * hold_d2[...]
+
+    def part(k):
+        return slice(k * width, (k + 1) * width)
+
+    for k in range(chunks):
+        copy2(k).wait()
+        mine, other = total1[k], take2[k].astype(F32)
+        d_late = jnp.where(low2, hold_d2[0:1, part(k)], both_d1[0:1, inner(ours + k)])
+        total2[k] = d_late * jnp.where(low2, mine, other) + jnp.where(low2, other, mine)
 
         @pl.when(link == 0)
         def _():
-            sendbuf[k] = total[k].astype(BF16)
-            send_copy(k).start()
+            sent[k] = total2[k].astype(BF16)
+            copy3(k).start()
+
+    def hand_over(k, into):
+        mine, other = s_ref[:, lanes(core, k)], take1[k].astype(F32)
+        d_early = jnp.where(low1, d_ref[0:1, lanes(core, k)], hold_d1[0:1, inner(k)])
+        passed = d_early * into + jnp.where(low1, mine, other)
+        in_ref[:, lanes(core, k)] = jnp.where(low1, into, passed).astype(BF16)
+        back1[k] = jnp.where(low1, passed, into).astype(BF16)
+        copy5(k).start()
 
     for k in range(chunks):
 
         @pl.when(link == 0)
         def _():
-            recvbuf[k] = jnp.zeros((STATE, width), BF16)
+            arrive[k] = jnp.zeros((STATE, width), BF16)
 
         @pl.when(link > 0)
         def _():
-            send_copy(k).wait_recv()
-
-        arrived = recvbuf[k].astype(F32)
+            copy3(k).wait_recv()
+
+        into = arrive[k].astype(F32)
 
         @pl.when((link > 0) & (link < links - 1))
         def _():
-            sendbuf[k] = (both_d[k, 0:1] * arrived + total[k]).astype(BF16)
-            send_copy(k).start()
-
-        mine, other = s_ref[:, piece(core, k)], theirs[k].astype(F32)
-        d_mine, d_other = d_ref[0:1, piece(core, k)], their_d[0:1, piece(core, k)]
-        passed = jnp.where(low, d_mine, d_other) * arrived + jnp.where(low, mine, other)
-        in_ref[:, piece(core, k)] = jnp.where(low, arrived, passed).astype(BF16)
-        back[k] = jnp.where(low, passed, arrived).astype(BF16)
-        back_copy(k).start()
-    for k in range(chunks):
-        back_copy(k).wait()
-        in_ref[:, piece(1 - core, k)] = backed[k]
+            sent[k] = (both_d2[0:1, part(k)] * into + total2[k]).astype(BF16)
+            copy3(k).start()
+
+        mine, other = total1[k], take2[k].astype(F32)
+        d_early = jnp.where(low2, both_d1[0:1, inner(ours + k)], hold_d2[0:1, part(k)])
+        passed = d_early * into + jnp.where(low2, mine, other)
+        back2[k] = jnp.where(low2, passed, into).astype(BF16)
+        copy4(k).start()
+        hand_over(ours + k, jnp.where(low2, into, passed))
+    for k in range(chunks):
+        copy4(k).wait()
+        hand_over(theirs + k, home2[k].astype(F32))
+    for k in order[chunks:] + order[:chunks]:
+        copy5(k).wait()
+        in_ref[:, lanes(1 - core, k)] = home1[k]
+    for k in range(chunks):
 
         @pl.when(link < links - 1)
         def _():
-            send_copy(k).wait_send()
+            copy3(k).wait_send()
 
 
 def output_kernel(
@@ -341,8 +400,8 @@
             jax.ShapeDtypeStruct((8, channels), F32),
         ],
         scratch_shapes=[
-            pltpu.VMEM((BLOCK + 8, channels), F32),
-            pltpu.VMEM((BLOCK + 8, pairs), F32),
+            pltpu.VMEM((TAIL + BLOCK, channels), BF16),
+            pltpu.VMEM((TAIL + BLOCK, pairs), BF16),
             pltpu.VMEM((BLOCK, channels), BF16),
             pltpu.VMEM((2 * repeat, wide), BF16),
         ],
@@ -353,20 +412,22 @@
         conv_x, bias_x[None], conv_bc, bias_bc,
     )
 
-    chunks = 16
-    width = channels // 2 // chunks
-    pieces = pltpu.VMEM((chunks, STATE, width), BF16)
-    sems = pltpu.SemaphoreType.DMA((chunks,))
+    chunks = max(1, min(8, channels // 4 // LANES))
+    quarter = channels // 4
+    width = quarter // chunks
+    ones, twos = (pltpu.VMEM((n * chunks, STATE, width), BF16) for n in (1, 2))
+    total = pltpu.VMEM((chunks, STATE, width), F32)
+    half_d, quarter_d = pltpu.VMEM((8, 2 * quarter), F32), pltpu.VMEM((8, quarter), F32)
+    sem_one, sem_two = (pltpu.SemaphoreType.DMA((n * chunks, 2)) for n in (1, 2))
     incoming = pl.pallas_call(
         functools.partial(chain_kernel, chunks),
         in_specs=[pl.BlockSpec(memory_space=pltpu.VMEM)] * 2,
         out_specs=pl.BlockSpec(memory_space=pltpu.VMEM),
         out_shape=jax.ShapeDtypeStruct((STATE, channels), BF16),
         scratch_shapes=[
-            pieces, pieces, pltpu.VMEM((8, channels), F32),
-            pltpu.VMEM((chunks, STATE, width), F32), pltpu.VMEM((chunks, 8, width), F32),
-            pieces, pieces, pieces, pieces,
-            sems, sems, sems, sems, sems, sems, pltpu.SemaphoreType.DMA((2,)),
+            twos, twos, ones, ones, total, total, ones, ones, ones, ones, twos, twos,
+            half_d, half_d, quarter_d, quarter_d,
+            sem_two, sem_one, sem_one, sem_one, sem_two, pltpu.SemaphoreType.DMA((2, 2)),
         ],
         compiler_params=pltpu.CompilerParams(
             collective_id=0, has_side_effects=True, vmem_limit_bytes=VMEM_LIMIT

time: 103 us -> 87.8 us (0.85); the launches traced: 103 us -> 86.6 us
  Pallas kernels: 96.4 us -> 79.9 us
    pallas_call x1, Pallas kernels: 43 us -> 30.5 us  [shards(): pl.pallas_call(functools.partial(chain_kernel, chunks), in_specs=[pl.Bloc...]
    pallas_call x1, Pallas kernels: 26.4 us -> 22.3 us  [shards(): pl.pallas_call(functools.partial(local_kernel, groups), grid=(blocks,), i...]
where the time goes in v2:
time: 87.8 us; the launch traced here: 86.6 us
  Pallas kernels  79.9 us (91%)
  local copies, waits for them, and re-layouts  5.37 us (6%)
  starting transfers between devices  1.29 us (1%)
    pallas_call x1, Pallas kernels, shards(): pl.pallas_call(functools.partial(chain_kernel, chunks), in_specs=[pl.Bloc...  30.5 us
    pallas_call x1, Pallas kernels, shards(): pl.pallas_call(functools.partial(output_kernel, groups), grid=(blocks,),...  27 us
    pallas_call x1, Pallas kernels, shards(): pl.pallas_call(functools.partial(local_kernel, groups), grid=(blocks,), i...  22.3 us
    unnamed x4, local copies, waits for them, and re-layouts  3.68 us
  transfers between devices with their start and end apart: 1, of which 0 were waited for; matrix products, arithmetic and copies ran while one was open for 3% of the time, Pallas kernels for 0%

profile of v2, /device:TPU:31, one launch (start us, length us, event | category | flops | bytes accessed | tf_op | source)
XLA Modules:
  0.0 86.6 jit_solution(9208677486733241250)
XLA Ops:
  0.0 0.8 slice.10
  0.8 0.9 %slice.9 = bf16[16,4096]{1,0:T(8,128)(2,1)S(1)} slice(bf16[768,4096]{1,0:T(8,128)(2,1)} %x_ref.1), slice={[752:768], [0:4096]} | slice | bytes 262144 | tf_op jit(solution)/shard_map/slice | solution.py:376
  1.7 1.3 %collective-permute-start = (bf16[16,5120]{1,0:T(8,128)(2,1)S(1)}, bf16[16,5120]{1,0:T(8,128)(2,1)S(1)}, u32[]{:S(2)}, u32[]{:S(2)}) collective-permute-start(bf16[16,5120]{1,0:T(8,128)(2,1)S(1)} %pad_maximum_fusion), channel_id=1, source_target_pairs={{0,2},{2,4},{4,6},{6,8},{8,10},{10,12},{12,14},{14,16},{16,18},{18... | collective-permute-start | bytes 491528 | tf_op jit(solution)/shard_map/ppermute | solution.py:377
  3.0 3.0 %copy.14 = bf16[96,8,4,256]{3,1,2,0:T(8,128)(2,1)} copy(bf16[96,8,4,256]{3,2,1,0:T(4,128)(2,1)} %bitcast.11) | data formatting | bytes 3145728
  6.0 0.0 collective-permute-done.tail_ref
  6.0 0.0 copy-start
  6.0 0.7 copy-done
  6.7 22.3 %local_state.1 = (bf16[768,4096]{1,0:T(8,128)(2,1)}, bf16[768,1024]{1,0:T(8,128)(2,1)}, f32[128,4096]{1,0:T(8,128)}, f32[8,4096]{1,0:T(8,128)}) custom-call(s32[4]{0:T(128)} %seg_ref.3, bf16[768,4096]{1,0:T(8,128)(2,1)} %x_ref.1, bf16[768,1024]{1,0:T(8,128)(2,1)} %bitcast.10, bf16[16,5120]{1,0:T(8,128)(2,1)} %copy-done, bf16[64,768]{1,0:T(8,128)(2,1)} %bitcast.12, ...), custom_call_target="tpu_custom_call" | custom-call | tf_op jit(solution)/shard_map/local_state/pallas_call | solution.py:387
  29.0 30.5 %state_chain.1.in_ref = bf16[128,4096]{1,0:T(8,128)(2,1)} custom-call(f32[128,4096]{1,0:T(8,128)} %get-tuple-element.11.s_ref, f32[8,4096]{1,0:T(8,128)} %get-tuple-element.12.d_ref), custom_call_target="tpu_custom_call" | custom-call | tf_op jit(solution)/shard_map/state_chain/pallas_call | solution.py:422
  59.6 27.0 %block_outputs.1 = bf16[768,4096]{1,0:T(8,128)(2,1)} custom-call(s32[4]{0:T(128)} %seg_ref.3, bf16[768,4096]{1,0:T(8,128)(2,1)} %get-tuple-element.9.xc_ref, bf16[768,1024]{1,0:T(8,128)(2,1)} %get-tuple-element.10.bcc_ref, bf16[768,4096]{1,0:T(8,128)(2,1)} %z_ref.1, bf16[128,4096]{1,0:T(8,128)(2,1)} %state_chain.1.in_ref, bf16[64,768]{1,0:T(8,128)(2,1)} %bitcast.13, ...), custom_call_target="tpu_custom_call" | custom-call | tf_op jit(solution)/shard_map/block_outputs/pallas_call | solution.py:439
  (2 shorter events, 0.0 us)
Async XLA Ops:
  1.7 4.3 %collective-permute-start = (bf16[16,5120]{1,0:T(8,128)(2,1)S(1)}, bf16[16,5120]{1,0:T(8,128)(2,1)S(1)}, u32[]{:S(2)}, u32[]{:S(2)}) collective-permute-start(bf16[16,5120]{1,0:T(8,128)(2,1)S(1)} %pad_maximum_fusion), channel_id=1, source_target_pairs={{0,2},{2,4},{4,6},{6,8},{8,10},{10,12},{12,14},{14,16},{16,18},{18... | collective-permute-start | bytes 491528 | tf_op jit(solution)/shard_map/ppermute | solution.py:377
  6.0 0.7 copy-start

commit v3 on v2

--- a/solution.py
+++ b/solution.py
@@ -12,6 +12,7 @@
 BLOCK = 128
 LANES = 128
 TAIL = 16
+CONV_LANES = 256
 VMEM_LIMIT = 60 << 20
 LOG2E = 1.4426950408889634
 MESH = pl.DeviceIdType.MESH
@@ -23,8 +24,8 @@
     return half + half * jnp.tanh(half)
 
 
-def mm(a, b, dims, precision=None):
-    return lax.dot_general(a, b, (dims, ((), ())), precision=precision, preferred_element_type=F32)
+def mm(a, b, dims):
+    return lax.dot_general(a, b, (dims, ((), ())), preferred_element_type=F32)
 
 
 def ids_of(starts, positions):
@@ -72,8 +73,14 @@
     la = (-LOG2E * column(jnp.exp(dec_ref[...]))) * dt
     s = lax.broadcasted_iota(jnp.int32, (BLOCK, BLOCK), 0)
     t = lax.broadcasted_iota(jnp.int32, (BLOCK, BLOCK), 1)
-    upper = (s <= t).astype(F32)
-    return dt, mm(la, upper, ((1,), (0,)), lax.Precision.HIGHEST)
+    upper = (s <= t).astype(F32).astype(BF16)
+    n = la.shape[0]
+    parts, rest = [], la
+    for _ in range(3):
+        parts.append(rest.astype(BF16))
+        rest = rest - parts[-1].astype(F32)
+    sums = mm(jnp.concatenate(parts, axis=0), upper, ((1,), (0,)))
+    return dt, sums[0:n] + (sums[n : 2 * n] + sums[2 * n : 3 * n])
 
 
 def fill_spread(e_ref):
@@ -115,7 +122,7 @@
 def local_kernel(
     groups, seg_ref, x_ref, bc_ref, tail_ref, dtp_ref, dtb_ref, dec_ref,
     wx_ref, bx_ref, wbc_ref, bbc_ref,
-    xc_ref, bcc_ref, s_ref, d_ref, xhalo, bhalo, scaled, e_ref,
+    xc_ref, bcc_ref, s_ref, d_ref, dt_ref, cum_ref, upd_ref, xhalo, bhalo, scaled, e_ref,
 ):
     b = pl.program_id(0)
     channels = x_ref.shape[1]
@@ -140,6 +147,8 @@
     spot = Spot(seg_ref, b)
     shift = shift_matrix(spot.tall - spot.tall_id)
     dt, cum = steps_of(dtp_ref, dtb_ref, dec_ref)
+    dt_ref[...] = dt
+    cum_ref[...] = cum
     last = cum[:, BLOCK - 1 : BLOCK]
     tail_weight = jnp.exp2(last - cum) * dt * spot.same_end
     end_decay = jnp.exp2(jnp.broadcast_to(last, cum.shape)) * spot.alive_end
@@ -150,14 +159,15 @@
         weights = [wbc_ref[k, g : g + 1, :] for k in range(4)]
         conv_tile(bcc_ref, bhalo, shift, sl, sl, weights, bbc_ref[g : g + 1, :])
         tailw = expand(tail_weight[heads], e_ref)
-        decay = expand(end_decay[heads], e_ref)[0:8]
-        for j in range(0, wide, 2 * LANES):
-            sl = slice(g * wide + j, g * wide + j + 2 * LANES)
+        decay = expand(end_decay[heads, 0:8], e_ref)
+        for j in range(0, wide, CONV_LANES):
+            sl = slice(g * wide + j, g * wide + j + CONV_LANES)
             weights = [wx_ref[k : k + 1, sl] for k in range(4)]
             value = conv_tile(xc_ref, xhalo, shift, sl, sl, weights, bx_ref[0:1, sl])
-            scaled[:, sl] = (value.astype(F32) * tailw[:, j : j + 2 * LANES]).astype(BF16)
+            scaled[:, sl] = (value.astype(F32) * tailw[:, j : j + CONV_LANES]).astype(BF16)
         b_part = bcc_ref[:, g * 2 * STATE : g * 2 * STATE + STATE]
         update = mm(b_part, scaled[:, lanes], ((0,), (0,)))
+        upd_ref[:, lanes] = update
         s_ref[:, lanes] = decay[0:1] * s_ref[:, lanes] + update
         d_ref[:, lanes] = decay * d_ref[:, lanes]
 
@@ -298,13 +308,13 @@
 
 
 def output_kernel(
-    groups, seg_ref, xc_ref, bcc_ref, z_ref, in_ref, dtp_ref, dtb_ref, dec_ref, skip_ref, gain_ref,
-    out_ref, state, cfac, scaled, carried, gated, skip_row, e_ref,
+    groups, seg_ref, xc_ref, bcc_ref, z_ref, in_ref, dt_ref, cum_ref, upd_ref, skip_ref, gain_ref,
+    out_ref, state, cfac, carried, gated, skip_row, e_ref,
 ):
     b = pl.program_id(0)
     channels = xc_ref.shape[1]
     wide = channels // groups
-    repeat = dtp_ref.shape[0] // groups
+    repeat = dt_ref.shape[0] // groups
 
     @pl.when(b == 0)
     def _():
@@ -316,10 +326,8 @@
             skip_row[:, g * wide : (g + 1) * wide] = expand(rows, e_ref)[0:8]
 
     spot = Spot(seg_ref, b)
-    dt, cum = steps_of(dtp_ref, dtb_ref, dec_ref)
+    dt, cum = dt_ref[...], cum_ref[...]
     carry_weight = jnp.exp2(cum) * spot.alive
-    last = cum[:, BLOCK - 1 : BLOCK]
-    tail_weight = jnp.exp2(last - cum) * dt * spot.same_end
     lower_rows = cum - jnp.log2(dt)
     columns = jnp.transpose(cum)
     t = lax.broadcasted_iota(jnp.int32, (BLOCK, BLOCK), 0)
@@ -331,7 +339,6 @@
         heads = slice(g * repeat, (g + 1) * repeat)
         lanes = slice(g * wide, (g + 1) * wide)
         cfac[:, lanes] = expand(carry_weight[heads], e_ref)
-        tailw = expand(tail_weight[heads], e_ref)
         b_part = bcc_ref[:, g * 2 * STATE : g * 2 * STATE + STATE]
         c_part = bcc_ref[:, g * 2 * STATE + STATE : (g + 1) * 2 * STATE]
         carried[:, lanes] = mm(c_part, state[:, lanes].astype(BF16), ((1,), (0,)))
@@ -347,7 +354,6 @@
             pair = jnp.concatenate([jnp.where(left, xc, none), jnp.where(left, none, xc)], axis=0)
             y = mm(jnp.concatenate(parts, axis=1), pair, ((1,), (0,)))
             xf = xc.astype(F32)
-            scaled[:, sl] = (xf * tailw[:, j * LANES : (j + 1) * LANES]).astype(BF16)
             full = y + cfac[:, sl] * carried[:, sl] + skip_row[0:1, sl] * xf
             held = full * silu_of_half(0.5 * z_ref[:, sl].astype(F32))
             gated[:, sl] = held
@@ -356,8 +362,7 @@
         scale = jnp.broadcast_to(lax.rsqrt(mean + 1e-05), (BLOCK, LANES))
         for sl in tiles(g * wide, wide):
             out_ref[:, sl] = (gated[:, sl] * scale * gain_ref[0:1, sl]).astype(BF16)
-        update = mm(b_part, scaled[:, lanes], ((0,), (0,)))
-        state[:, lanes] = cfac[BLOCK - 1 : BLOCK, lanes] * state[:, lanes] + update
+        state[:, lanes] = cfac[BLOCK - 1 : BLOCK, lanes] * state[:, lanes] + upd_ref[:, lanes]
 
 
 def shards(
@@ -379,12 +384,13 @@
     tall = lambda w: pl.BlockSpec((BLOCK, w), lambda b: (b, 0))
     whole = lambda *shape: pl.BlockSpec(shape, lambda b: (0,) * len(shape))
     lengths = pl.BlockSpec(memory_space=pltpu.SMEM)
-    scalars = [pl.BlockSpec((heads, BLOCK), lambda b: (0, b)), whole(1, heads), whole(1, heads)]
+    per_head = pl.BlockSpec((heads, BLOCK), lambda b: (0, b))
+    scalars = [per_head, whole(1, heads), whole(1, heads)]
     params = pltpu.CompilerParams(
         dimension_semantics=("arbitrary",), vmem_limit_bytes=VMEM_LIMIT
     )
     pairs = groups * 2 * STATE
-    xc, bcc, summary, decays = pl.pallas_call(
+    xc, bcc, summary, decays, dt, cum, updates = pl.pallas_call(
         functools.partial(local_kernel, groups),
         grid=(blocks,),
         in_specs=[
@@ -392,12 +398,18 @@
             whole(lookback + 1, channels), whole(1, channels),
             whole(lookback + 1, groups, 2 * STATE), whole(groups, 2 * STATE),
         ],
-        out_specs=[tall(channels), tall(pairs), whole(STATE, channels), whole(8, channels)],
+        out_specs=[
+            tall(channels), tall(pairs), whole(STATE, channels), whole(8, channels), per_head, per_head,
+            tall(channels),
+        ],
         out_shape=[
             jax.ShapeDtypeStruct((rows, channels), BF16),
             jax.ShapeDtypeStruct((rows, pairs), BF16),
             jax.ShapeDtypeStruct((STATE, channels), F32),
             jax.ShapeDtypeStruct((8, channels), F32),
+            jax.ShapeDtypeStruct((heads, rows), F32),
+            jax.ShapeDtypeStruct((heads, rows), F32),
+            jax.ShapeDtypeStruct((rows, channels), F32),
         ],
         scratch_shapes=[
             pltpu.VMEM((TAIL + BLOCK, channels), BF16),
@@ -440,20 +452,19 @@
         functools.partial(output_kernel, groups),
         grid=(blocks,),
         in_specs=[
-            lengths, tall(channels), tall(pairs), tall(channels), whole(STATE, channels), *scalars,
+            lengths, tall(channels), tall(pairs), tall(channels), whole(STATE, channels), per_head, per_head, tall(channels),
             whole(1, heads), whole(1, channels),
         ],
         out_specs=tall(channels),
         out_shape=jax.ShapeDtypeStruct((rows, channels), BF16),
         scratch_shapes=[
-            pltpu.VMEM((STATE, channels), F32), big, pltpu.VMEM((BLOCK, channels), BF16), big, big,
+            pltpu.VMEM((STATE, channels), F32), big, big, big,
             pltpu.VMEM((8, channels), F32), pltpu.VMEM((2 * repeat, wide), BF16),
         ],
         compiler_params=params,
         name="block_outputs",
     )(
-        seg_lengths, xc, bcc, z_gate, incoming, dtp, dt_bias[None], decay_log[None],
-        skip_gain[None], norm_gain[None],
+        seg_lengths, xc, bcc, z_gate, incoming, dt, cum, updates, skip_gain[None], norm_gain[None],
     )
 
 

time: 87.8 us -> 83.6 us (0.952)
  Pallas kernels: 79.9 us -> 75.8 us
    pallas_call x1, Pallas kernels: 27 us -> 24.1 us  [shards(): pl.pallas_call(functools.partial(output_kernel, groups), grid=(blocks,),...]
    pallas_call x1, Pallas kernels: 22.3 us -> 21.2 us  [shards(): pl.pallas_call(functools.partial(local_kernel, groups), grid=(blocks,), i...]
  transfers between devices with their start and end apart: 1 -> 1, of which waited for: 0 -> 0; matrix products, arithmetic and copies ran while one was open for 3% -> 4% of each run, Pallas kernels for 0% -> 0%
where the time goes in v3:
time: 83.6 us; the launch traced here: 82.5 us
  Pallas kernels  75.8 us (91%)
  local copies, waits for them, and re-layouts  5.29 us (6%)
  starting transfers between devices  1.29 us (2%)
    pallas_call x1, Pallas kernels, shards(): pl.pallas_call(functools.partial(chain_kernel, chunks), in_specs=[pl.Bloc...  30.5 us
    pallas_call x1, Pallas kernels, shards(): pl.pallas_call(functools.partial(output_kernel, groups), grid=(blocks,),...  24.1 us
    pallas_call x1, Pallas kernels, shards(): pl.pallas_call(functools.partial(local_kernel, groups), grid=(blocks,), i...  21.2 us
    unnamed x4, local copies, waits for them, and re-layouts  3.6 us
    slice x2, local copies, waits for them, and re-layouts, shards(): tails = jnp.concatenate([x_proj[rows - TAIL:], bc[rows - TAIL:]], axis=1)  1.69 us
  transfers between devices with their start and end apart: 1, of which 0 were waited for; matrix products, arithmetic and copies ran while one was open for 4% of the time, Pallas kernels for 0%

profile of v3, /device:TPU:31, one launch (start us, length us, event | category | flops | bytes accessed | tf_op | source)
XLA Modules:
  0.0 82.5 jit_solution(16271452979224135055)
XLA Ops:
  0.0 0.8 slice.10
  0.8 0.9 %slice.9 = bf16[16,4096]{1,0:T(8,128)(2,1)S(1)} slice(bf16[768,4096]{1,0:T(8,128)(2,1)} %x_ref.1), slice={[752:768], [0:4096]} | slice | bytes 262144 | tf_op jit(solution)/shard_map/slice | solution.py:381
  1.7 1.3 %collective-permute-start = (bf16[16,5120]{1,0:T(8,128)(2,1)S(1)}, bf16[16,5120]{1,0:T(8,128)(2,1)S(1)}, u32[]{:S(2)}, u32[]{:S(2)}) collective-permute-start(bf16[16,5120]{1,0:T(8,128)(2,1)S(1)} %pad_maximum_fusion), channel_id=1, source_target_pairs={{0,2},{2,4},{4,6},{6,8},{8,10},{10,12},{12,14},{14,16},{16,18},{18... | collective-permute-start | bytes 491528 | tf_op jit(solution)/shard_map/ppermute | solution.py:382
  3.0 2.9 %copy.14 = bf16[96,8,4,256]{3,1,2,0:T(8,128)(2,1)} copy(bf16[96,8,4,256]{3,2,1,0:T(4,128)(2,1)} %bitcast.11) | data formatting | bytes 3145728
  6.0 0.0 collective-permute-done.tail_ref
  6.0 0.0 copy-start
  6.0 0.7 copy-done
  6.6 21.2 %local_state.1 = (bf16[768,4096]{1,0:T(8,128)(2,1)}, bf16[768,1024]{1,0:T(8,128)(2,1)}, f32[128,4096]{1,0:T(8,128)}, f32[8,4096]{1,0:T(8,128)}, f32[64,768]{1,0:...) custom-call(s32[4]{0:T(128)} %seg_ref.3, bf16[768,4096]{1,0:T(8,128)(2,1)} %x_ref.1, bf16[768,1024]{1,0:T(8,128)(2,1)} %bitcast.10, ...), custom_call_target="tpu_custom_call" | custom-call | tf_op jit(solution)/shard_map/local_state/pallas_call | solution.py:393
  27.9 30.5 %state_chain.1.in_ref = bf16[128,4096]{1,0:T(8,128)(2,1)} custom-call(f32[128,4096]{1,0:T(8,128)} %get-tuple-element.14.s_ref, f32[8,4096]{1,0:T(8,128)} %get-tuple-element.15.d_ref), custom_call_target="tpu_custom_call" | custom-call | tf_op jit(solution)/shard_map/state_chain/pallas_call | solution.py:434
  58.3 24.1 %block_outputs.1 = bf16[768,4096]{1,0:T(8,128)(2,1)} custom-call(s32[4]{0:T(128)} %seg_ref.3, bf16[768,4096]{1,0:T(8,128)(2,1)} %get-tuple-element.12.xc_ref, bf16[768,1024]{1,0:T(8,128)(2,1)} %get-tuple-element.13.bcc_ref, bf16[768,4096]{1,0:T(8,128)(2,1)} %z_ref.1, bf16[128,4096]{1,0:T(8,128)(2,1)} %state_chain.1.in_ref, ...), custom_call_target="tpu_custom_call" | custom-call | tf_op jit(solution)/shard_map/block_outputs/pallas_call | solution.py:451
  (2 shorter events, 0.0 us)
Async XLA Ops:
  1.7 4.2 %collective-permute-start = (bf16[16,5120]{1,0:T(8,128)(2,1)S(1)}, bf16[16,5120]{1,0:T(8,128)(2,1)S(1)}, u32[]{:S(2)}, u32[]{:S(2)}) collective-permute-start(bf16[16,5120]{1,0:T(8,128)(2,1)S(1)} %pad_maximum_fusion), channel_id=1, source_target_pairs={{0,2},{2,4},{4,6},{6,8},{8,10},{10,12},{12,14},{14,16},{16,18},{18... | collective-permute-start | bytes 491528 | tf_op jit(solution)/shard_map/ppermute | solution.py:382
  6.0 0.7 copy-start
